TPU v7x, 32 devices: a whole 2x2x4 slice. The times are simulated.
32 devices in a mesh: trc: 4 (over z), lat: 4 (over y, x), lon: 2 (over core).
Axes of the slice: x: 2, y: 2, z: 4, core: 2. Of those that a mesh axis runs over, the one named last changes fastest.
Arguments:
- tracers: float32 [8, 16, 128, 128], P('trc', 'lat', 'lon'), may hold values from -6 to 6
- land_mask: int32 [16, 128], P('lat', 'lon'), may hold values 0 or 1
- bottom_level: int32 [16, 128], P('lat', 'lon'), may hold values from 1 to 128
- bottom_part: float32 [16, 128], P('lat', 'lon'), may hold values from 0.05 to 1
- velocity: float32 [2, 2, 8, 32768], P(None, None, ('lat', 'lon'), 'trc'), may hold values from -0.45 to 0.45
- upwelling: float32 [2, 8, 32768], P(None, ('lat', 'lon'), 'trc'), may hold values from -0.3 to 0.3
- diffusivity: float32 [2, 8, 32768], P(None, ('lat', 'lon'), 'trc'), may hold values from 0.08 to 0.32
Outputs:
- tracers_out: float32 [8, 16, 128, 128], P('trc', 'lat', 'lon')
All inputs are finite; a program needn't handle non-finite values. No bound on the sum of `land_mask` on one device may be relied on, other than what follows from the above.
Results may differ from a plain program's by a relative error of at most 0.0003.
Values sent between devices are 32-bit elements; how exact they have to be, the bound alone decides.
A program may use at most 64 MiB of HBM per device.

v0:
```python
import jax
import jax.numpy as jnp
from jax import lax
from jax.sharding import PartitionSpec as P

STEPS = 2


fraction_floor = 0.25


def with_halo(block, sides, width):
    for axis, dim in sides:
        count = lax.axis_size(axis)
        forward = [(i, i + 1) for i in range(count - 1)]
        backward = [(target, source) for source, target in forward]
        low = lax.ppermute(
            lax.slice_in_dim(block, block.shape[dim] - width, None, axis=dim), axis, forward
        )
        high = lax.ppermute(lax.slice_in_dim(block, 0, width, axis=dim), axis, backward)
        block = jnp.concatenate([low, block, high], axis=dim)
    return block


def minmod(first, second):
    return 0.5 * (jnp.sign(first) + jnp.sign(second)) * jnp.minimum(jnp.abs(first), jnp.abs(second))


def window(array, start, stop, offset):
    return lax.slice_in_dim(array, start, stop, axis=array.ndim + offset)


def face_divergence(field, speed, mixing, fraction, offset):
    extent = field.shape[field.ndim + offset]
    before = window(field, 0, extent - 3, offset)
    lower = window(field, 1, extent - 2, offset)
    upper = window(field, 2, extent - 1, offset)
    after = window(field, 3, extent, offset)
    face_speed = 0.5 * (window(speed, 1, extent - 2, offset) + window(speed, 2, extent - 1, offset))
    face_area = jnp.minimum(
        window(fraction, 1, extent - 2, offset), window(fraction, 2, extent - 1, offset)
    )
    face_mixing = 0.5 * (
        window(mixing, 1, extent - 2, offset) + window(mixing, 2, extent - 1, offset)
    )
    jump = upper - lower
    damping = 0.5 * (1.0 - jnp.abs(face_speed))
    from_lower = lower + damping * minmod(lower - before, jump)
    from_upper = upper - damping * minmod(jump, after - upper)
    face_value = jnp.where(face_speed >= 0.0, from_lower, from_upper)
    face_flux = face_area * (face_speed * face_value - face_mixing * jump)
    return window(face_flux, 1, extent - 3, offset) - window(face_flux, 0, extent - 4, offset)


def substep(field, fraction, eastward, northward, mixing, rising):
    across_rows = face_divergence(field, northward, mixing, fraction, -3)[..., 2:-2, :]
    across_cols = face_divergence(field, eastward, mixing, fraction, -2)[..., 2:-2, :, :]
    centre = field[..., 2:-2, 2:-2, :]
    wet_share = fraction[2:-2, 2:-2, :]
    top_area = jnp.minimum(wet_share[:, :, :-1], wet_share[:, :, 1:])
    lifting = rising[:, :, :-1]
    carried = jnp.where(lifting >= 0.0, centre[..., :-1], centre[..., 1:])
    vertical = top_area * lifting * carried
    closed = jnp.zeros(vertical.shape[:-1] + (1,), jnp.float32)
    across_levels = jnp.concatenate([vertical, closed], axis=-1) - jnp.concatenate(
        [closed, vertical], axis=-1
    )
    return centre - (across_rows + across_cols + across_levels) / jnp.maximum(
        wet_share, fraction_floor
    )


def cell_fraction(land_mask, bottom_level, bottom_part, levels):
    level_index = lax.broadcasted_iota(jnp.int32, land_mask.shape + (levels,), 2)
    deepest = bottom_level[:, :, None] - 1
    full_cell = (level_index < deepest).astype(jnp.float32)
    last_cell = (level_index == deepest).astype(jnp.float32) * bottom_part[:, :, None]
    return land_mask.astype(jnp.float32)[:, :, None] * (full_cell + last_cell)


def body(tracers, land_mask, bottom_level, bottom_part, velocity, upwelling, diffusivity):
    levels = tracers.shape[3]
    block_shape = (tracers.shape[1], tracers.shape[2], levels)
    fraction = cell_fraction(land_mask, bottom_level, bottom_part, levels)
    tracer_count = tracers.shape[0]
    collected = []
    moved = (
        lax.all_gather(velocity, "trc", axis=3, tiled=True),
        lax.all_gather(upwelling, "trc", axis=2, tiled=True),
        lax.all_gather(diffusivity, "trc", axis=2, tiled=True),
    )
    speeds = moved[0].reshape((STEPS, 2) + block_shape)
    rises = moved[1].reshape((STEPS,) + block_shape)
    mixes = moved[2].reshape((STEPS,) + block_shape)
    collected = [
        (speeds[number, 0], speeds[number, 1], mixes[number], rises[number])
        for number in range(STEPS)
    ]
    field = tracers
    wide_frac = fraction
    for number in range(STEPS):
        eastward, northward, mixing, rising = collected[number]
        extras = [fraction[None]] if number == 0 else []
        stack = jnp.concatenate(
            [field] + extras + [jnp.stack([eastward, northward, mixing])], axis=0
        )
        widened = with_halo(stack, (("lat", 1), ("lon", 2)), 2)
        if number == 0:
            wide_frac = widened[tracer_count]
            moved_flows = widened[tracer_count + 1 :]
        else:
            moved_flows = widened[tracer_count:]
        field = substep(
            widened[:tracer_count],
            wide_frac,
            moved_flows[0],
            moved_flows[1],
            moved_flows[2],
            rising,
        )
    return field


def solution(mesh):
    placed = (
        P("trc", "lat", "lon", None),
        P("lat", "lon"),
        P("lat", "lon"),
        P("lat", "lon"),
        P(None, None, ("lat", "lon"), "trc"),
        P(None, ("lat", "lon"), "trc"),
        P(None, ("lat", "lon"), "trc"),
    )
    return jax.shard_map(
        body, mesh=mesh, in_specs=placed, out_specs=P("trc", "lat", "lon", None), check_vma=False
    )
```

profile of v0, /device:TPU:0, one launch (start us, length us, event | category | flops | bytes accessed | tf_op | source)
XLA Modules:
  0.0 89.0 jit_solution(9641395497896303604)
XLA Ops:
  0.0 0.7 convert_element_type.14
  0.7 0.7 broadcast_add_fusion
  1.4 15.8 %all_gather.10 = f32[2,1,32768]{2,1,0:T(1,128)S(1)} all-gather(f32[2,1,8192]{2,1,0:T(1,128)} %param.13), channel_id=1, replica_groups=mesh['trc'=4,'lat'=4,'lon'=2] {'trc'}, dimensions={2}, use_global_device_ids=true | all-gather | bytes 327680 | tf_op jit(solution)/shard_map/all_gather | solution.py:90
  17.3 16.4 %all_gather.9 = f32[2,2,1,32768]{3,2,1,0:T(1,128)S(1)} all-gather(f32[2,2,1,8192]{3,2,1,0:T(1,128)} %param.11), channel_id=1, replica_groups=mesh['trc'=4,'lat'=4,'lon'=2] {'trc'}, dimensions={3}, use_global_device_ids=true | all-gather | bytes 655360 | tf_op jit(solution)/shard_map/all_gather | solution.py:88
  34.0 3.4 %collective-permute-start = (f32[6,2,64,128]{3,2,1,0:T(8,128)S(1)}, f32[6,2,64,128]{3,2,1,0:T(8,128)S(1)}, u32[]{:S(2)}, u32[]{:S(2)}) collective-permute-start(f32[6,2,64,128]{3,2,1,0:T(8,128)S(1)} %get-tuple-element.25), channel_id=1, source_target_pairs={{0,2},{2,4},{4,6},{1,3},{3,5},{5,7},{8,10},{10,12},{12,14},{9,11},... | collective-permute-start | bytes 1179656 | tf_op jit(solution)/shard_map/ppermute | solution.py:17
  37.4 1.3 %collective-permute-start.1 = (f32[6,2,64,128]{3,2,1,0:T(8,128)S(1)}, f32[6,2,64,128]{3,2,1,0:T(8,128)S(1)}, u32[]{:S(2)}, u32[]{:S(2)}) collective-permute-start(f32[6,2,64,128]{3,2,1,0:T(8,128)S(1)} %get-tuple-element.26), channel_id=1, source_target_pairs={{2,0},{4,2},{6,4},{3,1},{5,3},{7,5},{10,8},{12,10},{14,12},{11,9},... | collective-permute-start | bytes 1179656 | tf_op jit(solution)/shard_map/ppermute | solution.py:20
  38.8 13.8 %all_gather.11 = f32[2,1,32768]{2,1,0:T(1,128)S(1)} all-gather(f32[2,1,8192]{2,1,0:T(1,128)S(1)} %copy-done.1), channel_id=1, replica_groups=mesh['trc'=4,'lat'=4,'lon'=2] {'trc'}, dimensions={2}, use_global_device_ids=true | all-gather | bytes 327680 | tf_op jit(solution)/shard_map/all_gather | solution.py:89
  52.7 1.3 %collective-permute-start.2 = (f32[6,8,2,128]{3,2,1,0:T(2,128)S(1)}, f32[6,8,2,128]{3,2,1,0:T(2,128)S(1)}, u32[]{:S(2)}, u32[]{:S(2)}) collective-permute-start(f32[6,8,2,128]{3,2,1,0:T(2,128)S(1)} %get-tuple-element.16), channel_id=1, source_target_pairs={{0,1},{2,3},{4,5},{6,7},{8,9},{10,11},{12,13},{14,15},{16,17},{18,... | collective-permute-start | bytes 147464 | tf_op jit(solution)/shard_map/ppermute | solution.py:17
  54.0 1.3 %collective-permute-start.3 = (f32[6,8,2,128]{3,2,1,0:T(2,128)S(1)}, f32[6,8,2,128]{3,2,1,0:T(2,128)S(1)}, u32[]{:S(2)}, u32[]{:S(2)}) collective-permute-start(f32[6,8,2,128]{3,2,1,0:T(2,128)S(1)} %get-tuple-element.17), channel_id=1, source_target_pairs={{1,0},{3,2},{5,4},{7,6},{9,8},{11,10},{13,12},{15,14},{17,16},{19,... | collective-permute-start | bytes 147464 | tf_op jit(solution)/shard_map/ppermute | solution.py:20
  55.3 1.8 %collective-permute-done.3 = f32[6,8,2,128]{3,2,1,0:T(2,128)S(1)} collective-permute-done((f32[6,8,2,128]{3,2,1,0:T(2,128)S(1)}, f32[6,8,2,128]{3,2,1,0:T(2,128)S(1)}, u32[]{:S(2)}, u32[]{:S(2)}) %collective-permute-start.3) | collective-permute-done | bytes 49184 | tf_op jit(solution)/shard_map/ppermute | solution.py:20
  57.1 0.2 pad_maximum_fusion
  57.8 0.3 subtract_multiply_fusion.3
  58.3 1.0 %subtract_multiply_fusion.1 = f32[2,8,65,128]{3,2,1,0:T(8,128)S(1)} fusion(f32[6,8,2,128]{3,2,1,0:T(2,128)S(1)} %collective-permute-done.3, f32[6,2,64,128]{3,2,1,0:T(8,128)S(1)} %collective-permute-done.1, f32[6,4,64,128]{3,2,1,0:T(8,128)S(1)} %constant_dynamic-update-slice_fusion, f32[6,2,64,128]{3,2,1,0:T(8,128)S(1)} %collective-permute-done, ...), kind=kLoop, calls=%fused_computation.33 | loop fusion | flops 5058560 | bytes 3335168 | tf_op jit(solution)/shard_map/mul | solution.py:51
  59.6 0.2 fusion.24
  59.9 4.6 %collective-permute-start.4 = (f32[5,2,64,128]{3,2,1,0:T(8,128)S(1)}, f32[5,2,64,128]{3,2,1,0:T(8,128)S(1)}, u32[]{:S(2)}, u32[]{:S(2)}) collective-permute-start(f32[5,2,64,128]{3,2,1,0:T(8,128)S(1)} %get-tuple-element.27), channel_id=1, source_target_pairs={{0,2},{2,4},{4,6},{1,3},{3,5},{5,7},{8,10},{10,12},{12,14},{9,11},... | collective-permute-start | bytes 983048 | tf_op jit(solution)/shard_map/ppermute | solution.py:17
  64.5 1.3 %collective-permute-start.5 = (f32[5,2,64,128]{3,2,1,0:T(8,128)S(1)}, f32[5,2,64,128]{3,2,1,0:T(8,128)S(1)}, u32[]{:S(2)}, u32[]{:S(2)}) collective-permute-start(f32[5,2,64,128]{3,2,1,0:T(8,128)S(1)} %get-tuple-element.28), channel_id=1, source_target_pairs={{2,0},{4,2},{6,4},{3,1},{5,3},{7,5},{10,8},{12,10},{14,12},{11,9},... | collective-permute-start | bytes 983048 | tf_op jit(solution)/shard_map/ppermute | solution.py:20
  65.8 5.9 %collective-permute-done.4 = f32[5,2,64,128]{3,2,1,0:T(8,128)S(1)} collective-permute-done((f32[5,2,64,128]{3,2,1,0:T(8,128)S(1)}, f32[5,2,64,128]{3,2,1,0:T(8,128)S(1)}, u32[]{:S(2)}, u32[]{:S(2)}) %collective-permute-start.4) | collective-permute-done | bytes 327712 | tf_op jit(solution)/shard_map/ppermute | solution.py:17
  71.7 9.8 %collective-permute-done.5 = f32[5,2,64,128]{3,2,1,0:T(8,128)S(1)} collective-permute-done((f32[5,2,64,128]{3,2,1,0:T(8,128)S(1)}, f32[5,2,64,128]{3,2,1,0:T(8,128)S(1)}, u32[]{:S(2)}, u32[]{:S(2)}) %collective-permute-start.5) | collective-permute-done | bytes 327712 | tf_op jit(solution)/shard_map/ppermute | solution.py:20
  81.6 1.3 %collective-permute-start.6 = (f32[5,8,2,128]{3,2,1,0:T(2,128)S(1)}, f32[5,8,2,128]{3,2,1,0:T(2,128)S(1)}, u32[]{:S(2)}, u32[]{:S(2)}) collective-permute-start(f32[5,8,2,128]{3,2,1,0:T(2,128)S(1)} %get-tuple-element.23), channel_id=1, source_target_pairs={{0,1},{2,3},{4,5},{6,7},{8,9},{10,11},{12,13},{14,15},{16,17},{18,... | collective-permute-start | bytes 122888 | tf_op jit(solution)/shard_map/ppermute | solution.py:17
  82.9 1.3 %collective-permute-start.7 = (f32[5,8,2,128]{3,2,1,0:T(2,128)S(1)}, f32[5,8,2,128]{3,2,1,0:T(2,128)S(1)}, u32[]{:S(2)}, u32[]{:S(2)}) collective-permute-start(f32[5,8,2,128]{3,2,1,0:T(2,128)S(1)} %get-tuple-element.24), channel_id=1, source_target_pairs={{1,0},{3,2},{5,4},{7,6},{9,8},{11,10},{13,12},{15,14},{17,16},{19,... | collective-permute-start | bytes 122888 | tf_op jit(solution)/shard_map/ppermute | solution.py:20
  84.3 1.7 %collective-permute-done.7 = f32[5,8,2,128]{3,2,1,0:T(2,128)S(1)} collective-permute-done((f32[5,8,2,128]{3,2,1,0:T(2,128)S(1)}, f32[5,8,2,128]{3,2,1,0:T(2,128)S(1)}, u32[]{:S(2)}, u32[]{:S(2)}) %collective-permute-start.7) | collective-permute-done | bytes 40992 | tf_op jit(solution)/shard_map/ppermute | solution.py:20
  86.5 0.3 subtract_multiply_fusion.2
  87.0 1.0 %subtract_multiply_fusion = f32[2,8,65,128]{3,2,1,0:T(8,128)S(1)} fusion(f32[5,8,2,128]{3,2,1,0:T(2,128)S(1)} %collective-permute-done.7, f32[5,2,64,128]{3,2,1,0:T(8,128)S(1)} %collective-permute-done.5, f32[1,4,64,128]{3,2,1,0:T(8,128)S(1)} %bitcast.48, f32[1,4,64,128]{3,2,1,0:T(8,128)S(1)} %get-tuple-element.34, ...), kind=kLoop, calls=%fused_computation.29 | loop fusion | flops 6656000 | bytes 3056640 | tf_op jit(solution)/shard_map/mul | solution.py:51
  88.1 0.9 %fusion.20 = f32[2,4,64,128]{3,2,1,0:T(8,128)} fusion(f32[2,4,64,128]{3,2,1,0:T(8,128)S(1)} %fusion.24, f32[2,8,64,128]{3,2,1,0:T(8,128)S(1)} %get-tuple-element.30, f32[2,8,64,128]{3,2,1,0:T(8,128)S(1)} %get-tuple-element.29, f32[2,4,68,128]{3,2,1,0:T(8,128)S(1)} %get-tuple-element.36, f32[2,4,68,128]{3,2,1,0:T(8,128)S(1)} %get-tuple-element.35, ...), kind=kLoop, calls=%fused_computation.70 | loop fusion | flops 458752 | bytes 1964032 | tf_op jit(solution)/shard_map/sub | solution.py:68
  (46 shorter events, 2.1 us)
Async XLA Ops:
  0.0 33.7 %copy-start = (f32[2,4,64,128]{3,2,1,0:T(8,128)S(1)}, f32[2,4,64,128]{3,2,1,0:T(8,128)}, u32[]{:S(2)}) copy-start(f32[2,4,64,128]{3,2,1,0:T(8,128)} %param.7) | copy-start | bytes 786436
  0.0 33.7 %copy-start.2 = (f32[4,64]{1,0:T(4,128)S(1)}, f32[4,64]{1,0:T(4,128)}, u32[]{:S(2)}) copy-start(f32[4,64]{1,0:T(4,128)} %param.10) | copy-start | bytes 3076
  33.7 5.1 %copy-start.1 = (f32[2,1,8192]{2,1,0:T(1,128)S(1)}, f32[2,1,8192]{2,1,0:T(1,128)}, u32[]{:S(2)}) copy-start(f32[2,1,8192]{2,1,0:T(1,128)} %param.12) | copy-start | bytes 196612
  34.0 18.6 %collective-permute-start = (f32[6,2,64,128]{3,2,1,0:T(8,128)S(1)}, f32[6,2,64,128]{3,2,1,0:T(8,128)S(1)}, u32[]{:S(2)}, u32[]{:S(2)}) collective-permute-start(f32[6,2,64,128]{3,2,1,0:T(8,128)S(1)} %get-tuple-element.25), channel_id=1, source_target_pairs={{0,2},{2,4},{4,6},{1,3},{3,5},{5,7},{8,10},{10,12},{12,14},{9,11},... | collective-permute-start | bytes 1179656 | tf_op jit(solution)/shard_map/ppermute | solution.py:17
  37.4 15.2 %collective-permute-start.1 = (f32[6,2,64,128]{3,2,1,0:T(8,128)S(1)}, f32[6,2,64,128]{3,2,1,0:T(8,128)S(1)}, u32[]{:S(2)}, u32[]{:S(2)}) collective-permute-start(f32[6,2,64,128]{3,2,1,0:T(8,128)S(1)} %get-tuple-element.26), channel_id=1, source_target_pairs={{2,0},{4,2},{6,4},{3,1},{5,3},{7,5},{10,8},{12,10},{14,12},{11,9},... | collective-permute-start | bytes 1179656 | tf_op jit(solution)/shard_map/ppermute | solution.py:20
  52.7 2.6 %collective-permute-start.2 = (f32[6,8,2,128]{3,2,1,0:T(2,128)S(1)}, f32[6,8,2,128]{3,2,1,0:T(2,128)S(1)}, u32[]{:S(2)}, u32[]{:S(2)}) collective-permute-start(f32[6,8,2,128]{3,2,1,0:T(2,128)S(1)} %get-tuple-element.16), channel_id=1, source_target_pairs={{0,1},{2,3},{4,5},{6,7},{8,9},{10,11},{12,13},{14,15},{16,17},{18,... | collective-permute-start | bytes 147464 | tf_op jit(solution)/shard_map/ppermute | solution.py:17
  54.0 3.1 %collective-permute-start.3 = (f32[6,8,2,128]{3,2,1,0:T(2,128)S(1)}, f32[6,8,2,128]{3,2,1,0:T(2,128)S(1)}, u32[]{:S(2)}, u32[]{:S(2)}) collective-permute-start(f32[6,8,2,128]{3,2,1,0:T(2,128)S(1)} %get-tuple-element.17), channel_id=1, source_target_pairs={{1,0},{3,2},{5,4},{7,6},{9,8},{11,10},{13,12},{15,14},{17,16},{19,... | collective-permute-start | bytes 147464 | tf_op jit(solution)/shard_map/ppermute | solution.py:20
  59.9 11.8 %collective-permute-start.4 = (f32[5,2,64,128]{3,2,1,0:T(8,128)S(1)}, f32[5,2,64,128]{3,2,1,0:T(8,128)S(1)}, u32[]{:S(2)}, u32[]{:S(2)}) collective-permute-start(f32[5,2,64,128]{3,2,1,0:T(8,128)S(1)} %get-tuple-element.27), channel_id=1, source_target_pairs={{0,2},{2,4},{4,6},{1,3},{3,5},{5,7},{8,10},{10,12},{12,14},{9,11},... | collective-permute-start | bytes 983048 | tf_op jit(solution)/shard_map/ppermute | solution.py:17
  64.5 17.1 %collective-permute-start.5 = (f32[5,2,64,128]{3,2,1,0:T(8,128)S(1)}, f32[5,2,64,128]{3,2,1,0:T(8,128)S(1)}, u32[]{:S(2)}, u32[]{:S(2)}) collective-permute-start(f32[5,2,64,128]{3,2,1,0:T(8,128)S(1)} %get-tuple-element.28), channel_id=1, source_target_pairs={{2,0},{4,2},{6,4},{3,1},{5,3},{7,5},{10,8},{12,10},{14,12},{11,9},... | collective-permute-start | bytes 983048 | tf_op jit(solution)/shard_map/ppermute | solution.py:20
  81.6 2.7 %collective-permute-start.6 = (f32[5,8,2,128]{3,2,1,0:T(2,128)S(1)}, f32[5,8,2,128]{3,2,1,0:T(2,128)S(1)}, u32[]{:S(2)}, u32[]{:S(2)}) collective-permute-start(f32[5,8,2,128]{3,2,1,0:T(2,128)S(1)} %get-tuple-element.23), channel_id=1, source_target_pairs={{0,1},{2,3},{4,5},{6,7},{8,9},{10,11},{12,13},{14,15},{16,17},{18,... | collective-permute-start | bytes 122888 | tf_op jit(solution)/shard_map/ppermute | solution.py:17
  82.9 3.1 %collective-permute-start.7 = (f32[5,8,2,128]{3,2,1,0:T(2,128)S(1)}, f32[5,8,2,128]{3,2,1,0:T(2,128)S(1)}, u32[]{:S(2)}, u32[]{:S(2)}) collective-permute-start(f32[5,8,2,128]{3,2,1,0:T(2,128)S(1)} %get-tuple-element.24), channel_id=1, source_target_pairs={{1,0},{3,2},{5,4},{7,6},{9,8},{11,10},{13,12},{15,14},{17,16},{19,... | collective-permute-start | bytes 122888 | tf_op jit(solution)/shard_map/ppermute | solution.py:20
where the time goes:
time: 89.3 us; the launch traced here: 89 us
  blocking collectives  46 us (52%)
  waiting for transfers between devices  19.2 us (22%)
  starting transfers between devices  15.7 us (18%)
  other arithmetic  6.98 us (8%)
    all_gather x1, blocking collectives, body(): lax.all_gather(velocity, 'trc', axis=3, tiled=True)  16.4 us
    all_gather x1, blocking collectives, body(): lax.all_gather(diffusivity, 'trc', axis=2, tiled=True)  15.8 us
    all_gather x1, blocking collectives, body(): lax.all_gather(upwelling, 'trc', axis=2, tiled=True)  13.8 us
    ppermute x4, waiting for transfers between devices, with_halo(): lax.ppermute(lax.slice_in_dim(block, 0, width, axis=dim), axis, backward)  13.3 us
    ppermute x4, starting transfers between devices, with_halo(): lax.ppermute(lax.slice_in_dim(block, block.shape[dim] - width, None, axis...  10.6 us
    ppermute x4, waiting for transfers between devices, with_halo(): lax.ppermute(lax.slice_in_dim(block, block.shape[dim] - width, None, axis...  5.93 us
    ppermute x4, starting transfers between devices, with_halo(): lax.ppermute(lax.slice_in_dim(block, 0, width, axis=dim), axis, backward)  5.17 us
    mul x6, other arithmetic, face_divergence(): face_flux = face_area * (face_speed * face_value - face_mixing * jump)  2.82 us
  transfers between devices with their start and end apart: 8, of which 4 were waited for; matrix products, arithmetic and copies ran while one was open for 0% of the time, Pallas kernels for 0%

commit v1 on v0

--- a/solution.py
+++ b/solution.py
@@ -1,9 +1,14 @@
+import functools
+
 import jax
 import jax.numpy as jnp
 from jax import lax
+from jax.experimental import pallas as pl
+from jax.experimental.pallas import tpu as pltpu
 from jax.sharding import PartitionSpec as P
 
 STEPS = 2
+MESH = pl.DeviceIdType.MESH
 
 
 fraction_floor = 0.25
@@ -78,12 +83,11 @@
     return land_mask.astype(jnp.float32)[:, :, None] * (full_cell + last_cell)
 
 
-def body(tracers, land_mask, bottom_level, bottom_part, velocity, upwelling, diffusivity):
+def gathered_body(tracers, land_mask, bottom_level, bottom_part, velocity, upwelling, diffusivity):
     levels = tracers.shape[3]
     block_shape = (tracers.shape[1], tracers.shape[2], levels)
     fraction = cell_fraction(land_mask, bottom_level, bottom_part, levels)
     tracer_count = tracers.shape[0]
-    collected = []
     moved = (
         lax.all_gather(velocity, "trc", axis=3, tiled=True),
         lax.all_gather(upwelling, "trc", axis=2, tiled=True),
@@ -92,33 +96,362 @@
     speeds = moved[0].reshape((STEPS, 2) + block_shape)
     rises = moved[1].reshape((STEPS,) + block_shape)
     mixes = moved[2].reshape((STEPS,) + block_shape)
-    collected = [
-        (speeds[number, 0], speeds[number, 1], mixes[number], rises[number])
-        for number in range(STEPS)
-    ]
     field = tracers
     wide_frac = fraction
     for number in range(STEPS):
-        eastward, northward, mixing, rising = collected[number]
         extras = [fraction[None]] if number == 0 else []
         stack = jnp.concatenate(
-            [field] + extras + [jnp.stack([eastward, northward, mixing])], axis=0
+            [field] + extras + [jnp.stack([speeds[number, 0], speeds[number, 1], mixes[number]])],
+            axis=0,
         )
         widened = with_halo(stack, (("lat", 1), ("lon", 2)), 2)
         if number == 0:
             wide_frac = widened[tracer_count]
-            moved_flows = widened[tracer_count + 1 :]
+        flows = widened[-3:]
+        field = substep(
+            widened[:tracer_count], wide_frac, flows[0], flows[1], flows[2], rises[number]
+        )
+    return field
+
+
+U, K, V, W = range(4)
+PAD = 8
+CHUNK = 16
+
+
+def limited_flux(before, lower, upper, after, east, scale, area_speed, area_mix):
+    jump = upper - lower
+    base = jnp.where(east, lower, upper)
+    slope = jnp.where(east, lower - before, after - upper)
+    limited = jnp.maximum(jnp.minimum(slope, jump), 0.0) + jnp.minimum(
+        jnp.maximum(slope, jump), 0.0
+    )
+    return area_speed * (base + scale * limited) - area_mix * jump
+
+
+def face_terms(speed_p, speed_q, mix_p, mix_q, frac_p, frac_q):
+    speed = 0.5 * (speed_p + speed_q)
+    area = jnp.minimum(frac_p, frac_q)
+    east = speed >= 0.0
+    damping = 0.5 * (1.0 - jnp.abs(speed))
+    return east, jnp.where(east, damping, -damping), area * speed, area * (0.5 * (mix_p + mix_q))
+
+
+def transport_kernel(
+    counts, tr_hbm, vel_hbm, up_hbm, dif_hbm, mask_ref, level_ref, part_ref, out_ref,
+    c0, c1, flow, frac, rflux, xflux,
+    own_sem, in_sem, zs, zr, fs, cs, cr, fls, flr, frs, frr,
+):
+    n, n_lat, n_lon = counts
+    tracer_count, rows, cols, levels = tr_hbm.shape
+    t, la, lo = lax.axis_index("trc"), lax.axis_index("lat"), lax.axis_index("lon")
+    inner = pl.ds(PAD, cols)
+    left_halo, right_halo = pl.ds(0, PAD), pl.ds(PAD + cols, PAD)
+    left_edge, right_edge = pl.ds(PAD, PAD), pl.ds(cols, PAD)
+
+    sides = (
+        (la > 0, {"lat": la - 1}),
+        (la < n_lat - 1, {"lat": la + 1}),
+        (lo > 0, {"lon": lo - 1}),
+        (lo < n_lon - 1, {"lon": lo + 1}),
+    )
+    shifts = (1, -1, 2, -2)
+    groups = tuple(((t + d >= 0) & (t + d < n), {"trc": t + d}) for d in shifts)
+
+    barrier = pltpu.get_barrier_semaphore()
+    for there, device in sides + groups:
+        @pl.when(there)
+        def _(device=device):
+            pl.semaphore_signal(barrier, inc=1, device_id=device, device_id_type=MESH)
+    total = 0
+    for there, _ in sides + groups:
+        total = total + jnp.where(there, 1, 0)
+    pl.semaphore_wait(barrier, total)
+
+    def source(s, f):
+        return {
+            U: lambda: vel_hbm.at[s, 0], V: lambda: vel_hbm.at[s, 1],
+            K: lambda: dif_hbm.at[s], W: lambda: up_hbm.at[s],
+        }[f]()
+
+    def group_copy(s, f, i):
+        return pltpu.make_async_remote_copy(
+            src_ref=source(s, f), dst_ref=flow.at[s, f, 1 + t, inner],
+            send_sem=zs.at[s, f, i], recv_sem=zr.at[s, f, t],
+            device_id=groups[i][1], device_id_type=MESH,
+        )
+
+    def forward_copy(s, f, r, target):
+        return pltpu.make_async_remote_copy(
+            src_ref=flow.at[s, f, 1 + r, inner], dst_ref=flow.at[s, f, 1 + r, inner],
+            send_sem=fs.at[s, f], recv_sem=zr.at[s, f, r],
+            device_id={"trc": target}, device_id_type=MESH,
+        )
+
+    def own_copy(s, f):
+        return pltpu.make_async_copy(
+            source(s, f), flow.at[s, f, 1 + t, inner], own_sem.at[s, f]
+        )
+
+    def side_copy(src, dst, send, recv, i):
+        return pltpu.make_async_remote_copy(
+            src_ref=src, dst_ref=dst, send_sem=send.at[i], recv_sem=recv.at[i],
+            device_id=sides[i][1], device_id_type=MESH,
+        )
+
+    def field_copy(s, i):
+        dst = c0 if s == 0 else c1
+        if s == 0:
+            srcs = (
+                tr_hbm.at[:, pl.ds(0, 2)], tr_hbm.at[:, pl.ds(rows - 2, 2)],
+                tr_hbm.at[:, :, pl.ds(0, PAD)], tr_hbm.at[:, :, pl.ds(cols - PAD, PAD)],
+            )
         else:
-            moved_flows = widened[tracer_count:]
-        field = substep(
-            widened[:tracer_count],
-            wide_frac,
-            moved_flows[0],
-            moved_flows[1],
-            moved_flows[2],
-            rising,
-        )
-    return field
+            srcs = (
+                c1.at[:, pl.ds(2, 2), inner], c1.at[:, pl.ds(rows, 2), inner],
+                c1.at[:, pl.ds(2, rows), left_edge], c1.at[:, pl.ds(2, rows), right_edge],
+            )
+        dsts = (
+            dst.at[:, pl.ds(rows + 2, 2), inner], dst.at[:, pl.ds(0, 2), inner],
+            dst.at[:, pl.ds(2, rows), right_halo], dst.at[:, pl.ds(2, rows), left_halo],
+        )
+        return side_copy(srcs[i], dsts[i], cs.at[s], cr.at[s], i)
+
+    def frac_copy(i):
+        body = pl.ds(1, rows)
+        srcs = (frac.at[1, inner], frac.at[rows, inner],
+                frac.at[body, left_edge], frac.at[body, right_edge])
+        dsts = (frac.at[rows + 1, inner], frac.at[0, inner],
+                frac.at[body, right_halo], frac.at[body, left_halo])
+        return side_copy(srcs[i], dsts[i], frs, frr, i)
+
+    def flow_copy(s, i):
+        body = pl.ds(1, rows)
+        kv, uk = pl.ds(K, 2), pl.ds(U, 2)
+        srcs = (flow.at[s, kv, 1, inner], flow.at[s, kv, rows, inner],
+                flow.at[s, uk, body, left_edge], flow.at[s, uk, body, right_edge])
+        dsts = (flow.at[s, kv, rows + 1, inner], flow.at[s, kv, 0, inner],
+                flow.at[s, uk, body, right_halo], flow.at[s, uk, body, left_halo])
+        return side_copy(srcs[i], dsts[i], fls.at[s], flr.at[s], i)
+
+    opposite = (1, 0, 3, 2)
+
+    def on_sides(make, which, act):
+        for i in which:
+            @pl.when(sides[i][0])
+            def _(i=i):
+                getattr(make(i), act)()
+
+    def receive(make, which):
+        for i in which:
+            @pl.when(sides[opposite[i]][0])
+            def _(i=i):
+                make(i).wait_recv()
+
+    def start_group(s):
+        for f in (K, V, U, W):
+            for i in range(len(shifts)):
+                @pl.when(groups[i][0])
+                def _(f=f, i=i):
+                    group_copy(s, f, i).start()
+
+    start_group(0)
+    own_field = pltpu.make_async_copy(tr_hbm, c0.at[:, pl.ds(2, rows), inner], in_sem)
+    own_field.start()
+    for f in (K, V, U, W):
+        own_copy(0, f).start()
+    on_sides(functools.partial(field_copy, 0), range(4), "start")
+    start_group(1)
+    for f in (K, V, U, W):
+        own_copy(1, f).start()
+
+    square = (cols, cols)
+    eye = lax.broadcasted_iota(jnp.int32, square, 0) == lax.broadcasted_iota(jnp.int32, square, 1)
+    level = lax.broadcasted_iota(jnp.int32, (cols, levels), 1).astype(jnp.float32)
+
+    def upright(row):
+        return jnp.sum(jnp.where(eye, jnp.broadcast_to(row, square), 0.0), axis=1, keepdims=True)
+
+    for r in range(rows):
+        wet = mask_ref[r:r + 1, :].astype(jnp.float32)
+        deepest = upright(level_ref[r:r + 1, :].astype(jnp.float32) - 1.0)
+        share = upright(wet * part_ref[r:r + 1, :])
+        wet = upright(wet)
+        frac[1 + r, inner, :] = jnp.where(
+            level < deepest, wet, jnp.where(level == deepest, share, 0.0)
+        )
+    on_sides(frac_copy, range(4), "start")
+
+    @pl.when(la == 0)
+    def _():
+        for field in (c0, c1):
+            field[:, 0:2] = jnp.zeros((tracer_count, 2) + field.shape[2:], jnp.float32)
+        frac[0] = jnp.zeros(frac.shape[1:], jnp.float32)
+        flow[:, :, 0] = jnp.zeros((STEPS, 4) + flow.shape[3:], jnp.float32)
+
+    @pl.when(la == n_lat - 1)
+    def _():
+        for field in (c0, c1):
+            field[:, rows + 2:] = jnp.zeros((tracer_count, 2) + field.shape[2:], jnp.float32)
+        frac[rows + 1] = jnp.zeros(frac.shape[1:], jnp.float32)
+        flow[:, :, rows + 1] = jnp.zeros((STEPS, 4) + flow.shape[3:], jnp.float32)
+
+    for at_edge, strip in ((lo == 0, left_halo), (lo == n_lon - 1, right_halo)):
+        @pl.when(at_edge)
+        def _(strip=strip):
+            for field in (c0, c1):
+                field[:, 2:2 + rows, strip] = jnp.zeros(
+                    (tracer_count, rows, PAD, levels), jnp.float32)
+            frac[1:1 + rows, strip] = jnp.zeros((rows, PAD, levels), jnp.float32)
+            flow[:, :, 1:1 + rows, strip] = jnp.zeros((STEPS, 4, rows, PAD, levels), jnp.float32)
+
+    own_field.wait()
+    receive(frac_copy, range(4))
+
+    def arrive(s, f, r):
+        @pl.when(t == r)
+        def _():
+            own_copy(s, f).wait()
+
+        @pl.when(t != r)
+        def _():
+            forward_copy(s, f, r, t).wait_recv()
+
+    def collect(s):
+        for f in (K, V, U, W):
+            arrive(s, f, 0)
+
+            @pl.when(t == n - 2)
+            def _(f=f):
+                forward_copy(s, f, 0, n - 1).start()
+            arrive(s, f, n - 1)
+
+            @pl.when(t == 1)
+            def _(f=f):
+                forward_copy(s, f, n - 1, 0).start()
+            if f == V:
+                on_sides(functools.partial(flow_copy, s), (0, 1), "start")
+        for f in (K, V, U, W):
+            for r in range(1, n - 1):
+                arrive(s, f, r)
+        on_sides(functools.partial(flow_copy, s), (2, 3), "start")
+        receive(functools.partial(field_copy, s), range(4))
+        receive(functools.partial(flow_copy, s), range(4))
+
+    last_level = lax.broadcasted_iota(jnp.int32, (CHUNK, levels), 1) == levels - 1
+
+    def advance(s, src, write):
+        @pl.loop(0, rows + 1)
+        def _(i):
+            for c in range(0, cols, CHUNK):
+                at = pl.ds(PAD + c, CHUNK)
+                terms = face_terms(
+                    flow[s, V, i, at], flow[s, V, i + 1, at],
+                    flow[s, K, i, at], flow[s, K, i + 1, at], frac[i, at], frac[i + 1, at],
+                )
+                for a in range(tracer_count):
+                    rflux[a, i, pl.ds(c, CHUNK)] = limited_flux(
+                        src[a, i, at], src[a, i + 1, at], src[a, i + 2, at], src[a, i + 3, at],
+                        *terms,
+                    )
+
+        @pl.loop(0, rows)
+        def _(r):
+            for c, size in [(c, CHUNK) for c in range(0, cols, CHUNK)] + [(cols - 7, 8)]:
+                p, q = pl.ds(PAD + c - 1, size), pl.ds(PAD + c, size)
+                terms = face_terms(
+                    flow[s, U, r + 1, p], flow[s, U, r + 1, q],
+                    flow[s, K, r + 1, p], flow[s, K, r + 1, q], frac[r + 1, p], frac[r + 1, q],
+                )
+                for a in range(tracer_count):
+                    xflux[a, pl.ds(c, size)] = limited_flux(
+                        src[a, r + 2, pl.ds(PAD + c - 2, size)], src[a, r + 2, p],
+                        src[a, r + 2, q], src[a, r + 2, pl.ds(PAD + c + 1, size)], *terms,
+                    )
+            for c in range(0, cols, CHUNK):
+                at = pl.ds(PAD + c, CHUNK)
+                share = frac[r + 1, at]
+                rise = flow[s, W, r + 1, at]
+                area = jnp.where(
+                    last_level, 0.0, jnp.minimum(share, pltpu.roll(share, levels - 1, 1))
+                )
+                lifted = area * rise
+                upward = rise >= 0.0
+                inverse = 1.0 / jnp.maximum(share, fraction_floor)
+                for a in range(tracer_count):
+                    centre = src[a, r + 2, at]
+                    vertical = lifted * jnp.where(
+                        upward, centre, pltpu.roll(centre, levels - 1, 1)
+                    )
+                    net = (
+                        (rflux[a, r + 1, pl.ds(c, CHUNK)] - rflux[a, r, pl.ds(c, CHUNK)])
+                        + (xflux[a, pl.ds(c + 1, CHUNK)] - xflux[a, pl.ds(c, CHUNK)])
+                        + (vertical - pltpu.roll(vertical, 1, 1))
+                    )
+                    write(a, r, c, centre - net * inverse)
+
+    def write_middle(a, r, c, value):
+        c1[a, r + 2, pl.ds(PAD + c, CHUNK)] = value
+
+    def write_out(a, r, c, value):
+        out_ref[a, r, pl.ds(c, CHUNK)] = value
+
+    collect(0)
+    advance(0, c0, write_middle)
+    on_sides(functools.partial(field_copy, 1), range(4), "start")
+    collect(1)
+    advance(1, c1, write_out)
+
+    for s in range(STEPS):
+        for f in range(4):
+            for i in range(len(shifts)):
+                @pl.when(groups[i][0])
+                def _(s=s, f=f, i=i):
+                    group_copy(s, f, i).wait_send()
+
+            @pl.when((t == 1) | (t == n - 2))
+            def _(s=s, f=f):
+                forward_copy(s, f, 0, t).wait_send()
+        on_sides(functools.partial(field_copy, s), range(4), "wait_send")
+        on_sides(functools.partial(flow_copy, s), range(4), "wait_send")
+    on_sides(frac_copy, range(4), "wait_send")
+
+
+def fused_body(counts, tracers, land_mask, bottom_level, bottom_part, velocity, upwelling,
+               diffusivity):
+    tracer_count, rows, cols, levels = tracers.shape
+    wide = cols + 2 * PAD
+    row = (cols, levels)
+    dma = pltpu.SemaphoreType.DMA
+    hbm, vmem = pl.BlockSpec(memory_space=pl.ANY), pl.BlockSpec(memory_space=pltpu.VMEM)
+    return pl.pallas_call(
+        functools.partial(transport_kernel, counts),
+        out_shape=jax.ShapeDtypeStruct(tracers.shape, jnp.float32),
+        in_specs=[hbm] * 4 + [vmem] * 3,
+        out_specs=vmem,
+        scratch_shapes=[
+            pltpu.VMEM((tracer_count, rows + 4, wide, levels), jnp.float32),
+            pltpu.VMEM((tracer_count, rows + 4, wide, levels), jnp.float32),
+            pltpu.VMEM((STEPS, 4, rows + 2, wide, levels), jnp.float32),
+            pltpu.VMEM((rows + 2, wide, levels), jnp.float32),
+            pltpu.VMEM((tracer_count, rows + 1, cols, levels), jnp.float32),
+            pltpu.VMEM((tracer_count, cols + 8, levels), jnp.float32),
+            dma((STEPS, 4)), dma,
+            dma((STEPS, 4, 4)), dma((STEPS, 4, counts[0])), dma((STEPS, 4)),
+            dma((STEPS, 4)), dma((STEPS, 4)),
+            dma((STEPS, 4)), dma((STEPS, 4)),
+            dma((4,)), dma((4,)),
+        ],
+        compiler_params=pltpu.CompilerParams(
+            collective_id=0, has_side_effects=True, vmem_limit_bytes=32 * 1024 * 1024
+        ),
+    )(
+        tracers,
+        velocity.reshape((STEPS, 2) + row),
+        upwelling.reshape((STEPS,) + row),
+        diffusivity.reshape((STEPS,) + row),
+        land_mask, bottom_level, bottom_part,
+    )
 
 
 def solution(mesh):
@@ -131,6 +464,15 @@
         P(None, ("lat", "lon"), "trc"),
         P(None, ("lat", "lon"), "trc"),
     )
+    counts = tuple(mesh.shape[axis] for axis in ("trc", "lat", "lon"))
+
+    def body(*arrays):
+        tracers, velocity = arrays[0], arrays[4]
+        one_row = velocity.shape[3] == tracers.shape[2] * tracers.shape[3]
+        if counts[0] == 4 and tracers.shape[1] == 4 and one_row:
+            return fused_body(counts, *arrays)
+        return gathered_body(*arrays)
+
     return jax.shard_map(
         body, mesh=mesh, in_specs=placed, out_specs=P("trc", "lat", "lon", None), check_vma=False
     )

time: 89.3 us -> 38.7 us (0.43)
  blocking collectives: 46 us -> 0 us
  Pallas kernels: 0 us -> 32.7 us
  waiting for transfers between devices: 19.2 us -> 0 us
  starting transfers between devices: 15.7 us -> 0 us
  other arithmetic: 6.98 us -> 0 us
  local copies, waits for them, and re-layouts: 0.57 us -> 5.61 us
    all_gather x3 -> x0, blocking collectives: 46 us -> none  [the longest x1 16.4 us: body(): lax.all_gather(velocity, 'trc', axis=3, tiled=True)]
    pallas_call x0 -> x1, Pallas kernels: none -> 32.7 us  [fused_body(): pl.pallas_call(functools.partial(transport_kernel, counts), out_shape=jax...]
    ppermute x8 -> x0, waiting for transfers between devices: 19.2 us -> none  [the longest x4 13.3 us: with_halo(): lax.ppermute(lax.slice_in_dim(block, 0, width, axis=dim), axis, backward)]
    ppermute x8 -> x0, starting transfers between devices: 15.7 us -> none  [the longest x4 10.6 us: with_halo(): lax.ppermute(lax.slice_in_dim(block, block.shape[dim] - width, None, axis...]
    unnamed x9 -> x15, local copies, waits for them, and re-layouts: 0.05 us -> 5.61 us
    mul x13 -> x0, other arithmetic: 3.46 us -> none  [the longest x6 2.82 us: face_divergence(): face_flux = face_area * (face_speed * face_value - face_mixing * jump)]
    sub x3 -> x0, other arithmetic: 1.76 us -> none  [the longest x2 1.07 us: substep(): centre - (across_rows + across_cols + across_levels) / jnp.maximum(wet_sh...]
  transfers between devices with their start and end apart: 8 -> 0, of which waited for: 4 -> 0; matrix products, arithmetic and copies ran while one was open for 0% -> 0% of each run, Pallas kernels for 0% -> 0%
where the time goes in v1:
time: 38.7 us; the launch traced here: 38.4 us
  Pallas kernels  32.7 us (84%)
  local copies, waits for them, and re-layouts  5.61 us (14%)
    pallas_call x1, Pallas kernels, fused_body(): pl.pallas_call(functools.partial(transport_kernel, counts), out_shape=jax...  32.7 us
    unnamed x15, local copies, waits for them, and re-layouts  5.61 us

profile of v1, /device:TPU:0, one launch (start us, length us, event | category | flops | bytes accessed | tf_op | source)
XLA Modules:
  0.0 38.4 jit_solution(2760821451067122068)
XLA Ops:
  0.0 0.0 copy-start.5
  0.0 0.0 copy-start.4
  0.0 0.7 %copy-done.5 = s32[4,64]{1,0:T(4,128)S(1)} copy-done((s32[4,64]{1,0:T(4,128)S(1)}, s32[4,64]{1,0:T(4,128)}, u32[]{:S(2)}) %copy-start.5) | copy-done | bytes 1048
  0.7 0.0 copy-done.4
  0.7 0.0 copy-start
  0.7 0.9 %copy-done = f32[2,4,64,128]{3,2,1,0:T(8,128)S(1)} copy-done((f32[2,4,64,128]{3,2,1,0:T(8,128)S(1)}, f32[2,4,64,128]{3,2,1,0:T(8,128)}, u32[]{:S(2)}) %copy-start) | copy-done | bytes 262168
  1.6 0.0 copy-start.1
  1.7 0.9 %copy-done.1 = f32[2,2,1,8192]{3,2,1,0:T(1,128)S(1)} copy-done((f32[2,2,1,8192]{3,2,1,0:T(1,128)S(1)}, f32[2,2,1,8192]{3,2,1,0:T(1,128)}, u32[]{:S(2)}) %copy-start.1) | copy-done | bytes 131096
  2.6 0.0 copy-start.2
  2.6 0.8 %copy-done.2 = f32[2,1,8192]{2,1,0:T(1,128)S(1)} copy-done((f32[2,1,8192]{2,1,0:T(1,128)S(1)}, f32[2,1,8192]{2,1,0:T(1,128)}, u32[]{:S(2)}) %copy-start.2) | copy-done | bytes 65560
  3.4 0.0 copy-start.3
  3.4 0.8 %copy-done.3 = f32[2,1,8192]{2,1,0:T(1,128)S(1)} copy-done((f32[2,1,8192]{2,1,0:T(1,128)S(1)}, f32[2,1,8192]{2,1,0:T(1,128)}, u32[]{:S(2)}) %copy-start.3) | copy-done | bytes 65560
  4.2 0.0 copy-start.6
  4.2 0.7 %copy-done.6 = f32[4,64]{1,0:T(4,128)S(1)} copy-done((f32[4,64]{1,0:T(4,128)S(1)}, f32[4,64]{1,0:T(4,128)}, u32[]{:S(2)}) %copy-start.6) | copy-done | bytes 1048
  4.9 32.7 %shard_map.73 = f32[2,4,64,128]{3,2,1,0:T(8,128)S(1)} custom-call(f32[2,4,64,128]{3,2,1,0:T(8,128)S(1)} %copy-done, f32[2,2,64,128]{3,2,1,0:T(8,128)S(1)} %bitcast.3, f32[2,64,128]{2,1,0:T(8,128)S(1)} %bitcast.4, f32[2,64,128]{2,1,0:T(8,128)S(1)} %bitcast.5, s32[4,64]{1,0:T(4,128)S(1)} %copy-done.4, s32[4,64]{1,0:T(4,128)S(1)} %copy-done.5, ...), custom_call_target="tpu_custom_call" | custom-call | tf_op jit(solution)/shard_map/pallas_call | solution.py:427
  37.7 0.7 %copy.9 = f32[2,4,64,128]{3,2,1,0:T(8,128)} copy(f32[2,4,64,128]{3,2,1,0:T(8,128)S(1)} %shard_map.73) | data formatting | bytes 524288
Async XLA Ops:
  0.0 0.7 %copy-start.5 = (s32[4,64]{1,0:T(4,128)S(1)}, s32[4,64]{1,0:T(4,128)}, u32[]{:S(2)}) copy-start(s32[4,64]{1,0:T(4,128)} %level_ref.1) | copy-start | bytes 3076
  0.0 0.7 %copy-start.4 = (s32[4,64]{1,0:T(4,128)S(1)}, s32[4,64]{1,0:T(4,128)}, u32[]{:S(2)}) copy-start(s32[4,64]{1,0:T(4,128)} %mask_ref.1) | copy-start | bytes 3076
  0.7 0.9 %copy-start = (f32[2,4,64,128]{3,2,1,0:T(8,128)S(1)}, f32[2,4,64,128]{3,2,1,0:T(8,128)}, u32[]{:S(2)}) copy-start(f32[2,4,64,128]{3,2,1,0:T(8,128)} %tr_hbm.1) | copy-start | bytes 786436
  1.6 0.9 %copy-start.1 = (f32[2,2,1,8192]{3,2,1,0:T(1,128)S(1)}, f32[2,2,1,8192]{3,2,1,0:T(1,128)}, u32[]{:S(2)}) copy-start(f32[2,2,1,8192]{3,2,1,0:T(1,128)} %param.11) | copy-start | bytes 393220
  2.6 0.8 %copy-start.2 = (f32[2,1,8192]{2,1,0:T(1,128)S(1)}, f32[2,1,8192]{2,1,0:T(1,128)}, u32[]{:S(2)}) copy-start(f32[2,1,8192]{2,1,0:T(1,128)} %param.12) | copy-start | bytes 196612
  3.4 0.8 %copy-start.3 = (f32[2,1,8192]{2,1,0:T(1,128)S(1)}, f32[2,1,8192]{2,1,0:T(1,128)}, u32[]{:S(2)}) copy-start(f32[2,1,8192]{2,1,0:T(1,128)} %param.13) | copy-start | bytes 196612
  4.2 0.7 %copy-start.6 = (f32[4,64]{1,0:T(4,128)S(1)}, f32[4,64]{1,0:T(4,128)}, u32[]{:S(2)}) copy-start(f32[4,64]{1,0:T(4,128)} %part_ref.1) | copy-start | bytes 3076

commit v2 on v1

--- a/solution.py
+++ b/solution.py
@@ -138,9 +138,9 @@
 
 
 def transport_kernel(
-    counts, tr_hbm, vel_hbm, up_hbm, dif_hbm, mask_ref, level_ref, part_ref, out_ref,
-    c0, c1, flow, frac, rflux, xflux,
-    own_sem, in_sem, zs, zr, fs, cs, cr, fls, flr, frs, frr,
+    counts, tr_hbm, vel_hbm, up_hbm, dif_hbm, mask_hbm, level_hbm, part_hbm, out_ref,
+    c0, c1, flow, frac, rflux, xflux, mask_ref, level_ref, part_ref,
+    own_sem, in_sem, column_sem, zs, zr, fs, cs, cr, fls, flr, frs, frr,
 ):
     n, n_lat, n_lon = counts
     tracer_count, rows, cols, levels = tr_hbm.shape
@@ -155,16 +155,28 @@
         (lo > 0, {"lon": lo - 1}),
         (lo < n_lon - 1, {"lon": lo + 1}),
     )
-    shifts = (1, -1, 2, -2)
-    groups = tuple(((t + d >= 0) & (t + d < n), {"trc": t + d}) for d in shifts)
-
+    shifts = (2, -2, 1, -1)
+    groups = (
+        (t < n - 2, {"trc": t + 2}), (t >= 2, {"trc": t - 2}),
+        (t < n - 1, {"trc": t + 1}), (t > 0, {"trc": t - 1}),
+    )
+    relays = ((t == n - 2, n - 1, (0,)), (t == 1, 0, (n - 1,)))
+
+    columns = [
+        pltpu.make_async_copy(src, dst, column_sem.at[i])
+        for i, (src, dst) in enumerate(
+            ((mask_hbm, mask_ref), (level_hbm, level_ref), (part_hbm, part_ref)))
+    ]
+    for copy in columns:
+        copy.start()
     barrier = pltpu.get_barrier_semaphore()
-    for there, device in sides + groups:
+    partners = sides + groups
+    for there, device in partners:
         @pl.when(there)
         def _(device=device):
             pl.semaphore_signal(barrier, inc=1, device_id=device, device_id_type=MESH)
     total = 0
-    for there, _ in sides + groups:
+    for there, _ in partners:
         total = total + jnp.where(there, 1, 0)
     pl.semaphore_wait(barrier, total)
 
@@ -181,10 +193,10 @@
             device_id=groups[i][1], device_id_type=MESH,
         )
 
-    def forward_copy(s, f, r, target):
+    def forward_copy(s, f, r, target, slot=0):
         return pltpu.make_async_remote_copy(
             src_ref=flow.at[s, f, 1 + r, inner], dst_ref=flow.at[s, f, 1 + r, inner],
-            send_sem=fs.at[s, f], recv_sem=zr.at[s, f, r],
+            send_sem=fs.at[s, f, slot], recv_sem=zr.at[s, f, r],
             device_id={"trc": target}, device_id_type=MESH,
         )
 
@@ -261,6 +273,7 @@
     for f in (K, V, U, W):
         own_copy(0, f).start()
     on_sides(functools.partial(field_copy, 0), range(4), "start")
+
     start_group(1)
     for f in (K, V, U, W):
         own_copy(1, f).start()
@@ -272,6 +285,8 @@
     def upright(row):
         return jnp.sum(jnp.where(eye, jnp.broadcast_to(row, square), 0.0), axis=1, keepdims=True)
 
+    for copy in columns:
+        copy.wait()
     for r in range(rows):
         wet = mask_ref[r:r + 1, :].astype(jnp.float32)
         deepest = upright(level_ref[r:r + 1, :].astype(jnp.float32) - 1.0)
@@ -313,28 +328,35 @@
         def _():
             own_copy(s, f).wait()
 
-        @pl.when(t != r)
+        relayed = ((t == n - 2) & (r == 0)) | ((t == 1) & (r == n - 1))
+
+        @pl.when((t != r) & jnp.logical_not(relayed))
         def _():
             forward_copy(s, f, r, t).wait_recv()
 
+    def relay(s, f):
+        for here, target, sources in relays:
+            @pl.when(here)
+            def _(target=target, sources=sources):
+                for slot, r in enumerate(sources):
+                    forward_copy(s, f, r, t).wait_recv()
+                    forward_copy(s, f, r, target, slot).start()
+
     def collect(s):
-        for f in (K, V, U, W):
-            arrive(s, f, 0)
-
-            @pl.when(t == n - 2)
-            def _(f=f):
-                forward_copy(s, f, 0, n - 1).start()
-            arrive(s, f, n - 1)
-
-            @pl.when(t == 1)
-            def _(f=f):
-                forward_copy(s, f, n - 1, 0).start()
-            if f == V:
-                on_sides(functools.partial(flow_copy, s), (0, 1), "start")
-        for f in (K, V, U, W):
-            for r in range(1, n - 1):
+        for f in (K, V):
+            relay(s, f)
+        for f in (K, V):
+            for r in (0, n - 1):
+                arrive(s, f, r)
+        on_sides(functools.partial(flow_copy, s), (0, 1), "start")
+        for f in (U, W):
+            relay(s, f)
+        for f, those in ((K, (1, 2)), (V, (1, 2)), (U, (1, 2, 0, 3))):
+            for r in those:
                 arrive(s, f, r)
         on_sides(functools.partial(flow_copy, s), (2, 3), "start")
+        for r in range(n):
+            arrive(s, W, r)
         receive(functools.partial(field_copy, s), range(4))
         receive(functools.partial(flow_copy, s), range(4))
 
@@ -411,7 +433,8 @@
 
             @pl.when((t == 1) | (t == n - 2))
             def _(s=s, f=f):
-                forward_copy(s, f, 0, t).wait_send()
+                for slot in range(1):
+                    forward_copy(s, f, 0, t, slot).wait_send()
         on_sides(functools.partial(field_copy, s), range(4), "wait_send")
         on_sides(functools.partial(flow_copy, s), range(4), "wait_send")
     on_sides(frac_copy, range(4), "wait_send")
@@ -423,11 +446,11 @@
     wide = cols + 2 * PAD
     row = (cols, levels)
     dma = pltpu.SemaphoreType.DMA
-    hbm, vmem = pl.BlockSpec(memory_space=pl.ANY), pl.BlockSpec(memory_space=pltpu.VMEM)
+    hbm, vmem = pl.BlockSpec(memory_space=pltpu.HBM), pl.BlockSpec(memory_space=pltpu.VMEM)
     return pl.pallas_call(
         functools.partial(transport_kernel, counts),
         out_shape=jax.ShapeDtypeStruct(tracers.shape, jnp.float32),
-        in_specs=[hbm] * 4 + [vmem] * 3,
+        in_specs=[hbm] * 7,
         out_specs=vmem,
         scratch_shapes=[
             pltpu.VMEM((tracer_count, rows + 4, wide, levels), jnp.float32),
@@ -436,14 +459,17 @@
             pltpu.VMEM((rows + 2, wide, levels), jnp.float32),
             pltpu.VMEM((tracer_count, rows + 1, cols, levels), jnp.float32),
             pltpu.VMEM((tracer_count, cols + 8, levels), jnp.float32),
-            dma((STEPS, 4)), dma,
-            dma((STEPS, 4, 4)), dma((STEPS, 4, counts[0])), dma((STEPS, 4)),
+            pltpu.VMEM((rows, cols), jnp.int32),
+            pltpu.VMEM((rows, cols), jnp.int32),
+            pltpu.VMEM((rows, cols), jnp.float32),
+            dma((STEPS, 4)), dma, dma((3,)),
+            dma((STEPS, 4, 4)), dma((STEPS, 4, counts[0])), dma((STEPS, 4, 2)),
             dma((STEPS, 4)), dma((STEPS, 4)),
             dma((STEPS, 4)), dma((STEPS, 4)),
             dma((4,)), dma((4,)),
         ],
         compiler_params=pltpu.CompilerParams(
-            collective_id=0, has_side_effects=True, vmem_limit_bytes=32 * 1024 * 1024
+            collective_id=0, has_side_effects=True, vmem_limit_bytes=60 * 1024 * 1024
         ),
     )(
         tracers,

time: 38.7 us -> 34.5 us (0.89)
  local copies, waits for them, and re-layouts: 5.61 us -> 1.67 us
    unnamed x15 -> x1, local copies, waits for them, and re-layouts: 5.61 us -> 1.67 us
where the time goes in v2:
time: 34.5 us; the launch traced here: 34.3 us
  Pallas kernels  32.6 us (94%)
  local copies, waits for them, and re-layouts  1.67 us (5%)
    pallas_call x1, Pallas kernels, fused_body(): pl.pallas_call(functools.partial(transport_kernel, counts), out_shape=jax...  32.6 us
    unnamed x1, local copies, waits for them, and re-layouts  1.67 us

profile of v2, /device:TPU:0, one launch (start us, length us, event | category | flops | bytes accessed | tf_op | source)
XLA Modules:
  0.0 34.3 jit_solution(4739783567791643257)
XLA Ops:
  0.0 32.6 %shard_map.73 = f32[2,4,64,128]{3,2,1,0:T(8,128)} custom-call(f32[2,4,64,128]{3,2,1,0:T(8,128)} %tr_hbm.1, f32[2,2,64,128]{3,2,1,0:T(8,128)} %bitcast.3, f32[2,64,128]{2,1,0:T(8,128)} %bitcast.4, f32[2,64,128]{2,1,0:T(8,128)} %bitcast.5, s32[4,64]{1,0:T(4,128)} %mask_hbm.1, s32[4,64]{1,0:T(4,128)} %level_hbm.1, f32[4,64]{1,0:T(4,128)} %part_hbm.1), custom_call_target="tpu_custom_call" | custom-call | tf_op jit(solution)/shard_map/pallas_call | solution.py:450
  32.6 1.7 %copy.9 = f32[2,4,64,128]{3,2,1,0:T(8,128)} copy(f32[2,4,64,128]{3,2,1,0:T(8,128)} %shard_map.73) | data formatting | bytes 524288

commit v3 on v2

--- a/solution.py
+++ b/solution.py
@@ -175,10 +175,6 @@
         @pl.when(there)
         def _(device=device):
             pl.semaphore_signal(barrier, inc=1, device_id=device, device_id_type=MESH)
-    total = 0
-    for there, _ in partners:
-        total = total + jnp.where(there, 1, 0)
-    pl.semaphore_wait(barrier, total)
 
     def source(s, f):
         return {
@@ -260,21 +256,20 @@
             def _(i=i):
                 make(i).wait_recv()
 
-    def start_group(s):
-        for f in (K, V, U, W):
-            for i in range(len(shifts)):
-                @pl.when(groups[i][0])
+    def send_rows(s, fields, slots, when=None):
+        for f in fields:
+            for i in slots:
+                @pl.when(groups[i][0] if when is None else groups[i][0] & when)
                 def _(f=f, i=i):
                     group_copy(s, f, i).start()
 
-    start_group(0)
+    far, near = (0, 1), (2, 3)
+    ends = (t == 0) | (t == n - 1)
+    middle = jnp.logical_not(ends)
     own_field = pltpu.make_async_copy(tr_hbm, c0.at[:, pl.ds(2, rows), inner], in_sem)
     own_field.start()
     for f in (K, V, U, W):
         own_copy(0, f).start()
-    on_sides(functools.partial(field_copy, 0), range(4), "start")
-
-    start_group(1)
     for f in (K, V, U, W):
         own_copy(1, f).start()
 
@@ -295,7 +290,6 @@
         frac[1 + r, inner, :] = jnp.where(
             level < deepest, wet, jnp.where(level == deepest, share, 0.0)
         )
-    on_sides(frac_copy, range(4), "start")
 
     @pl.when(la == 0)
     def _():
@@ -320,6 +314,19 @@
             frac[1:1 + rows, strip] = jnp.zeros((rows, PAD, levels), jnp.float32)
             flow[:, :, 1:1 + rows, strip] = jnp.zeros((STEPS, 4, rows, PAD, levels), jnp.float32)
 
+    total = 0
+    for there, _ in partners:
+        total = total + jnp.where(there, 1, 0)
+    pl.semaphore_wait(barrier, total)
+
+    on_sides(frac_copy, range(4), "start")
+    on_sides(functools.partial(field_copy, 0), range(4), "start")
+    send_rows(0, (K, V), far + near)
+    send_rows(1, (K, V), far + near, ends)
+    send_rows(0, (U, W), far + near)
+    send_rows(1, (K, V), near + far, middle)
+    send_rows(1, (U, W), far + near)
+
     own_field.wait()
     receive(frac_copy, range(4))
 
@@ -342,21 +349,21 @@
                     forward_copy(s, f, r, t).wait_recv()
                     forward_copy(s, f, r, target, slot).start()
 
-    def collect(s):
-        for f in (K, V):
-            relay(s, f)
+    def edge_rows(s):
         for f in (K, V):
             for r in (0, n - 1):
                 arrive(s, f, r)
         on_sides(functools.partial(flow_copy, s), (0, 1), "start")
-        for f in (U, W):
-            relay(s, f)
+
+    def mixed_columns(s):
         for f, those in ((K, (1, 2)), (V, (1, 2)), (U, (1, 2, 0, 3))):
             for r in those:
                 arrive(s, f, r)
         on_sides(functools.partial(flow_copy, s), (2, 3), "start")
         for r in range(n):
             arrive(s, W, r)
+
+    def collect_halos(s):
         receive(functools.partial(field_copy, s), range(4))
         receive(functools.partial(flow_copy, s), range(4))
 
@@ -418,10 +425,22 @@
     def write_out(a, r, c, value):
         out_ref[a, r, pl.ds(c, CHUNK)] = value
 
-    collect(0)
+    for f in (K, V):
+        relay(0, f)
+    edge_rows(0)
+    for f in (K, V):
+        relay(1, f)
+    relay(0, U)
+    relay(0, W)
+    edge_rows(1)
+    mixed_columns(0)
+    collect_halos(0)
     advance(0, c0, write_middle)
     on_sides(functools.partial(field_copy, 1), range(4), "start")
-    collect(1)
+    for f in (U, W):
+        relay(1, f)
+    mixed_columns(1)
+    collect_halos(1)
     advance(1, c1, write_out)
 
     for s in range(STEPS):

time: 34.5 us -> 32.6 us (0.945)
  the two profiles are of different devices: /device:TPU:0 before, /device:TPU:4 now
where the time goes in v3:
time: 32.6 us; the launch traced here: 32.4 us
  Pallas kernels  30.7 us (94%)
  local copies, waits for them, and re-layouts  1.67 us (5%)
    pallas_call x1, Pallas kernels, fused_body(): pl.pallas_call(functools.partial(transport_kernel, counts), out_shape=jax...  30.7 us
    unnamed x1, local copies, waits for them, and re-layouts  1.67 us

profile of v3, /device:TPU:4, one launch (start us, length us, event | category | flops | bytes accessed | tf_op | source)
XLA Modules:
  0.0 32.4 jit_solution(10532806950804098293)
XLA Ops:
  0.0 30.7 %shard_map.73 = f32[2,4,64,128]{3,2,1,0:T(8,128)} custom-call(f32[2,4,64,128]{3,2,1,0:T(8,128)} %tr_hbm.1, f32[2,2,64,128]{3,2,1,0:T(8,128)} %bitcast.3, f32[2,64,128]{2,1,0:T(8,128)} %bitcast.4, f32[2,64,128]{2,1,0:T(8,128)} %bitcast.5, s32[4,64]{1,0:T(4,128)} %mask_hbm.1, s32[4,64]{1,0:T(4,128)} %level_hbm.1, f32[4,64]{1,0:T(4,128)} %part_hbm.1), custom_call_target="tpu_custom_call" | custom-call | tf_op jit(solution)/shard_map/pallas_call | solution.py:469
  30.7 1.7 %copy.9 = f32[2,4,64,128]{3,2,1,0:T(8,128)} copy(f32[2,4,64,128]{3,2,1,0:T(8,128)} %shard_map.73) | data formatting | bytes 524288

commit v4 on v3

--- a/solution.py
+++ b/solution.py
@@ -325,7 +325,7 @@
     send_rows(1, (K, V), far + near, ends)
     send_rows(0, (U, W), far + near)
     send_rows(1, (K, V), near + far, middle)
-    send_rows(1, (U, W), far + near)
+    send_rows(1, (U, W), far + near, ends)
 
     own_field.wait()
     receive(frac_copy, range(4))
@@ -436,6 +436,7 @@
     mixed_columns(0)
     collect_halos(0)
     advance(0, c0, write_middle)
+    send_rows(1, (U, W), far + near, middle)
     on_sides(functools.partial(field_copy, 1), range(4), "start")
     for f in (U, W):
         relay(1, f)

time: 32.6 us -> 30.8 us (0.945)
  the two profiles are of different devices: /device:TPU:4 before, /device:TPU:0 now
where the time goes in v4:
time: 30.8 us; the launch traced here: 30.7 us
  Pallas kernels  29 us (94%)
  local copies, waits for them, and re-layouts  1.67 us (5%)
    pallas_call x1, Pallas kernels, fused_body(): pl.pallas_call(functools.partial(transport_kernel, counts), out_shape=jax...  29 us
    unnamed x1, local copies, waits for them, and re-layouts  1.67 us

profile of v4, /device:TPU:0, one launch (start us, length us, event | category | flops | bytes accessed | tf_op | source)
XLA Modules:
  0.0 30.7 jit_solution(14559471000238794830)
XLA Ops:
  0.0 29.0 %shard_map.73 = f32[2,4,64,128]{3,2,1,0:T(8,128)} custom-call(f32[2,4,64,128]{3,2,1,0:T(8,128)} %tr_hbm.1, f32[2,2,64,128]{3,2,1,0:T(8,128)} %bitcast.3, f32[2,64,128]{2,1,0:T(8,128)} %bitcast.4, f32[2,64,128]{2,1,0:T(8,128)} %bitcast.5, s32[4,64]{1,0:T(4,128)} %mask_hbm.1, s32[4,64]{1,0:T(4,128)} %level_hbm.1, f32[4,64]{1,0:T(4,128)} %part_hbm.1), custom_call_target="tpu_custom_call" | custom-call | tf_op jit(solution)/shard_map/pallas_call | solution.py:470
  29.0 1.7 %copy.9 = f32[2,4,64,128]{3,2,1,0:T(8,128)} copy(f32[2,4,64,128]{3,2,1,0:T(8,128)} %shard_map.73) | data formatting | bytes 524288
